TPU v7x, 32 devices: a whole 2x2x4 slice. The times are simulated.
32 devices in a mesh: layer: 4 (over y, core), row: 4 (over z), col: 2 (over x).
Axes of the slice: x: 2, y: 2, z: 4, core: 2. Of those that a mesh axis runs over, the one named last changes fastest.
Arguments:
- edge_weight: bfloat16 [2048, 2048], P('row', 'col'), may hold values from 0 to 1, as said below
Outputs:
- clustering: float32 [4, 512], P('row', ('layer', 'col'))
Inputs may be any that keep to these rules, and one draw needn't show every extreme that they name: `edge_weight`: symmetric with a zero diagonal; every vertex v is linked to v - 1 and v + 1 (modulo 2048); an edge's entry lies in [0.2, 1], all other entries are 0.
All inputs are finite; a program needn't handle non-finite values.
Results may differ from a plain program's by a relative error of at most 0.0003.
Values may be sent and summed in bfloat16 or wider, within the bound.
A program may use at most 64 MiB of HBM per device.

v0:
```python
import jax
import jax.numpy as jnp
from jax import lax
from jax.sharding import PartitionSpec as P

STRIPE = 128


def local(edge_weight):
    layers = lax.axis_size("layer")
    layer_index = lax.axis_index("layer")
    row_count, col_count = edge_weight.shape
    row_global = lax.axis_index("row") * row_count + jnp.arange(row_count, dtype=jnp.int32)
    col_global = lax.axis_index("col") * col_count + jnp.arange(col_count, dtype=jnp.int32)
    lower = jnp.where(
        row_global[:, None] > col_global[None, :], edge_weight, jnp.zeros_like(edge_weight)
    )
    column_groups = lower.reshape(row_count, col_count // (STRIPE * layers), layers, STRIPE)
    left_local = lax.dynamic_index_in_dim(column_groups, layer_index, 2, keepdims=False).reshape(
        row_count, col_count // layers
    )
    row_groups = lower.reshape(row_count // (STRIPE * layers), layers, STRIPE, col_count)
    right_local = lax.dynamic_index_in_dim(row_groups, layer_index, 1, keepdims=False).reshape(
        row_count // layers, col_count
    )
    left_whole = lax.all_gather(left_local, "col", axis=1, tiled=True)
    right_whole = lax.all_gather(right_local, "row", axis=0, tiled=True)
    paths = jnp.dot(left_whole, right_whole, preferred_element_type=jnp.float32)
    triangles = jnp.sum(paths * lower, axis=1)
    degree = jnp.sum(jnp.where(left_local > 0, 1.0, 0.0).astype(jnp.float32), axis=1)
    layer_share = (
        lax.psum_scatter(triangles, "layer", scatter_dimension=0, tiled=True),
        lax.psum_scatter(degree, "layer", scatter_dimension=0, tiled=True),
    )
    tri_total, degree_total = (
        lax.psum_scatter(layer_share[0], "col", scatter_dimension=0, tiled=True),
        lax.psum_scatter(layer_share[1], "col", scatter_dimension=0, tiled=True),
    )
    clustering = 2.0 * tri_total / jnp.maximum(degree_total * (degree_total - 1.0), 2.0)
    return clustering.reshape(1, -1)


def solution(mesh):
    placed = (P("row", "col"),)
    return jax.shard_map(
        local, mesh=mesh, in_specs=placed, out_specs=P("row", ("layer", "col")), check_vma=False
    )
```

profile of v0, /device:TPU:0, one launch (start us, length us, event | category | flops | bytes accessed | tf_op | source)
XLA Modules:
  0.0 60.3 jit_solution(14782072480402922622)
XLA Ops:
  6.5 0.0 all-gather.3.cloned.1.call-start
  6.5 1.5 %compare_select_fusion = bf16[512,1024]{1,0:T(8,128)(2,1)S(1)} fusion(bf16[512,1024]{1,0:T(8,128)(2,1)} %param.1, s32[1024]{0:T(1024)S(1)} %iota_add_fusion, s32[512]{0:T(512)S(1)} %iota_add_fusion.1), kind=kLoop, calls=%fused_computation.1 | loop fusion | flops 1048576 | bytes 2103296 | tf_op jit(solution)/shard_map/jit(_where)/select_n | solution.py:15
  8.1 0.7 %constant_dynamic-slice_fusion = bf16[1,1,128,1024]{3,2,1,0:T(8,128)(2,1)} fusion(bf16[1,4,128,1024]{3,2,1,0:T(8,128)(2,1)S(1)} %bitcast.10, s32[]{:T(128)S(6)} %select_n.16), kind=kLoop, calls=%fused_computation.10 | loop fusion | bytes 524292 | tf_op jit(solution)/shard_map/jit(dynamic_index_in_dim)/dynamic_slice | solution.py:23
  8.8 0.0 all-gather.3.cloned.1.call-update
  8.8 0.8 %reshape.25 = bf16[512,2,4,128]{3,2,1,0:T(4,128)(2,1)S(1)} reshape(bf16[512,1024]{1,0:T(8,128)(2,1)S(1)} %compare_select_fusion) | data formatting | bytes 2097152 | tf_op jit(solution)/shard_map/reshape | solution.py:18
  9.6 0.0 copy-start.1
  9.6 0.0 copy-start
  9.7 0.5 constant_dynamic-slice_fusion.1
  10.2 0.7 %copy.4 = bf16[512,2,1,128]{0,3,1,2:T(8,128)(2,1)S(1)} copy(bf16[512,2,1,128]{3,2,1,0:T(2,128)(2,1)S(1)} %constant_dynamic-slice_fusion.1) | data formatting | bytes 524288
  10.9 0.0 copy-done.1
  10.9 0.6 dynamic-slice
  11.5 0.0 copy-done
  11.5 0.6 %dynamic-slice.2 = u32[1]{0:T(128)} dynamic-slice(u32[32]{0:T(128)S(1)} %copy-done, u32[]{:T(128)S(6)} %add.41), dynamic_slice_sizes={1} | dynamic-slice | bytes 12
  13.4 9.9 %all_gather.6 = bf16[512,512]{0,1:T(8,128)(2,1)S(1)} all-gather(bf16[512,256]{0,1:T(8,128)(2,1)S(1)} %bitcast.11), channel_id=1, replica_groups=mesh['layer'=4,'row'=4,'col'=2] {'col'}, dimensions={1}, use_global_device_ids=true | all-gather | bytes 786432 | tf_op jit(solution)/shard_map/all_gather | solution.py:26
  23.3 0.1 select_reduce_fusion
  23.4 16.3 %all-gather.3.cloned.1.call-done = bf16[1,1,512,1024]{3,2,1,0:T(8,128)(2,1)} async-done(((bf16[1,1,128,1024]{3,2,1,0:T(8,128)(2,1)}), bf16[1,1,512,1024]{3,2,1,0:T(8,128)(2,1)}) %all-gather.3.cloned.1.call-update) | async-done | bytes 1048592 | tf_op jit(solution)/shard_map/all_gather | solution.py:27
  39.7 2.0 %multiply_reduce_fusion = f32[512]{0:T(512)S(1)} fusion(bf16[512,1024]{1,0:T(8,128)(2,1)S(1)} %compare_select_fusion, bf16[512,512]{0,1:T(8,128)(2,1)S(1)} %all_gather.6, bf16[1,1,512,1024]{3,2,1,0:T(8,128)(2,1)} %all-gather.3.cloned.1.call-done), kind=kOutput, calls=%fused_computation | convolution fusion | flops 538443264 | bytes 2623488 | tf_op jit(solution)/shard_map/dot_general | solution.py:28
  41.7 6.1 %all-reduce.4 = (f32[512]{0:T(512)S(1)}, f32[512]{0:T(512)S(1)}) all-reduce(f32[512]{0:T(512)S(1)} %select_reduce_fusion, f32[512]{0:T(512)S(1)} %multiply_reduce_fusion), channel_id=5, replica_groups=mesh['layer'=4,'row'=4,'col'=2] {'layer'}, use_global_device_ids=true, to_apply=%region_4.5.clone | all-reduce | flops 1024 | bytes 8192
  47.8 0.1 dynamic-slice.5
  47.9 0.1 dynamic-slice.1
  48.0 4.9 %all-reduce.5 = (f32[128]{0:T(128)S(1)}, f32[128]{0:T(128)S(1)}) all-reduce(f32[128]{0:T(128)S(1)} %dynamic-slice.5, f32[128]{0:T(128)S(1)} %dynamic-slice.1), channel_id=6, replica_groups=mesh['layer'=4,'row'=4,'col'=2] {'col'}, use_global_device_ids=true, to_apply=%region_5.6.clone | all-reduce | flops 256 | bytes 2048
  52.9 0.6 fusion.3
  (2 shorter events, 0.0 us)
Async XLA Ops:
  6.5 33.2 %all-gather.3.cloned.1.call-start = ((), (), s32[]{:S(2)}) async-start(), calls=%async_computation | async-start | bytes 1310720 | tf_op jit(solution)/shard_map/all_gather | solution.py:27
  9.6 1.3 %copy-start.1 = (u32[32]{0:T(128)S(1)}, u32[32]{0:T(128)}, u32[]{:S(2)}) copy-start(u32[32]{0:T(128)} %constant.39) | copy-start | bytes 388
  9.6 1.9 %copy-start = (u32[32]{0:T(128)S(1)}, u32[32]{0:T(128)}, u32[]{:S(2)}) copy-start(u32[32]{0:T(128)} %constant.43) | copy-start | bytes 388
Sparse Core Ops, SparseCore 0:
  9.0 30.6 all-gather.2
where the time goes:
time: 60.6 us; the launch traced here: 60.3 us
  blocking collectives  20.9 us (34%)
  waiting for transfers between devices  16.3 us (27%)
  between operations  14.7 us (24%)
  local copies, waits for them, and re-layouts  4.1 us (7%)
  other arithmetic  2.22 us (4%)
  matrix products  2.04 us (3%)
    all_gather x1, waiting for transfers between devices, local(): right_whole = lax.all_gather(right_local, 'row', axis=0, tiled=True)  16.3 us
    unnamed x2, blocking collectives  11 us
    all_gather x1, blocking collectives, local(): left_whole = lax.all_gather(left_local, 'col', axis=1, tiled=True)  9.94 us
    unnamed x9, local copies, waits for them, and re-layouts  2.05 us
    dot_general x1, matrix products, local(): paths = jnp.dot(left_whole, right_whole, preferred_element_type=jnp.float32)  2.04 us
    select_n x1, other arithmetic, local(): jnp.where(row_global[:, None] > col_global[None, :], edge_weight, jnp.zer...  1.53 us
  transfers between devices with their start and end apart: 1, of which 1 were waited for; matrix products, arithmetic and copies ran while one was open for 5% of the time, Pallas kernels for 0%

commit v1 on v0

v1 whole, which is shorter than its diff:
```python
import functools

import jax
import jax.numpy as jnp
from jax import lax
from jax.experimental import pallas as pl
from jax.experimental.pallas import tpu as pltpu
from jax.sharding import PartitionSpec as P

STRIPE = 128
MESH = pl.DeviceIdType.MESH


def at(layer, row, col):
    return {"layer": layer, "row": row, "col": col}


def kernel(
    layers, rows, cols, w_ref, out_ref,
    block, mask_block, side, across, left, right, stage, cross_stage, column_sum, inbox,
    load_sem, keep_side_sem, keep_across_sem, keep_inbox_sem, side_send, side_recv,
    across_send, across_recv, plane_send, cross_send, inbox_recv,
):
    span = rows // cols
    m, n = w_ref.shape
    q = m // layers
    layer, row, col = (lax.axis_index(a) for a in ("layer", "row", "col"))
    group = row // span
    place = row % span
    above = col > group

    barrier = pltpu.get_barrier_semaphore()

    def greet(l, r, c):
        pl.semaphore_signal(barrier, inc=1, device_id=at(l, r, c), device_id_type=MESH)

    for l in range(layers):
        for c in range(cols):
            @pl.when(jnp.logical_or(l != layer, c != col))
            def _():
                greet(l, row, c)
    for s in range(span):
        @pl.when(s != place)
        def _():
            greet(layer, group * span + s, col)

    @pl.when(above)
    def _():
        for s in range(span):
            for l in range(layers):
                for c in range(cols):
                    greet(l, col * span + s, c)
    for r in range(rows):
        @pl.when(r < group * span)
        def _():
            for l in range(layers):
                greet(l, r, group)

    load = pltpu.make_async_copy(w_ref, block, load_sem)
    load.start()

    def side_source(s):
        return w_ref.at[:, pl.ds(pl.multiple_of(s * m + layer * q, q), q)]

    def side_slot(s):
        return side.at[:, pl.ds(s * q, q)]

    def across_slot(s):
        return across.at[pl.ds(pl.multiple_of(s * q, q), q), :]

    across_source = w_ref.at[pl.ds(pl.multiple_of(layer * q, q), q), :]
    keep_across = pltpu.make_async_copy(across_source, across_slot(place), keep_across_sem)
    keep_across.start()

    def keep_side(s):
        return pltpu.make_async_copy(side_source(s), side_slot(s), keep_side_sem.at[s])

    for s in range(span):
        @pl.when(s > place)
        def _():
            side[:, s * q:(s + 1) * q] = jnp.zeros((m, q), side.dtype)
            across[s * q:(s + 1) * q, :] = jnp.zeros((q, n), across.dtype)

        @pl.when(jnp.logical_and(col == group, s <= place))
        def _():
            keep_side(s).start()

    everyone = layers * cols - 1 + span - 1 + group * span * layers
    pl.semaphore_wait(barrier, everyone + jnp.where(above, span * layers * cols, 0))

    def side_copy(s, c):
        return pltpu.make_async_remote_copy(
            src_ref=side_source(s), dst_ref=side_slot(s), send_sem=side_send.at[s, c], recv_sem=side_recv.at[s],
            device_id=at(layer, row, c), device_id_type=MESH)

    def across_copy(s):
        return pltpu.make_async_remote_copy(
            src_ref=across_source, dst_ref=across_slot(place), send_sem=across_send.at[s],
            recv_sem=across_recv.at[place], device_id=at(layer, group * span + s, col), device_id_type=MESH)

    def side_sends(act):
        for s in range(span):
            for c in range(cols):
                @pl.when(jnp.logical_and(jnp.logical_and(col == group, c != col), s <= place))
                def _():
                    act(side_copy(s, c))

    def across_sends(act):
        for s in range(span):
            @pl.when(s > place)
            def _():
                act(across_copy(s))

    across_sends(lambda copy: copy.start())
    side_sends(lambda copy: copy.start())

    load.wait()
    per_layer = n // layers
    row_here = row * m + lax.broadcasted_iota(jnp.int32, (q, 1), 0)
    col_here = col * n + lax.broadcasted_iota(jnp.int32, (1, n), 1)
    for k in range(layers):
        held = block[k * q:(k + 1) * q, :].astype(jnp.float32)
        lower = row_here + k * q > col_here
        mask_block[k * q:(k + 1) * q, :] = jnp.where(jnp.logical_or(lower, above), held, 0.0)
        mine = col_here // per_layer == col * layers + layer
        linked = jnp.where(jnp.logical_and(jnp.logical_and(lower, held > 0), mine), 1.0, 0.0)
        counts = sum(linked[:, t:t + q] for t in range(0, n, q))
        stage[k, 1:2, :] = jnp.sum(counts.T, axis=0, keepdims=True)

    keep_across.wait()
    for s in range(span):
        @pl.when(jnp.logical_and(col == group, s <= place))
        def _():
            keep_side(s).wait()

        @pl.when(jnp.logical_and(col != group, s <= place))
        def _():
            side_copy(s, 0).wait_recv()
        inner = (group * span + s) * m + layer * q
        outer_rows = row * m + lax.broadcasted_iota(jnp.int32, (m, 1), 0)
        inner_cols = inner + lax.broadcasted_iota(jnp.int32, (1, q), 1)
        held = side[:, s * q:(s + 1) * q].astype(jnp.float32)
        left[:, s * q:(s + 1) * q] = jnp.where(outer_rows > inner_cols, held, 0.0).astype(left.dtype)
    for s in range(span):
        @pl.when(s < place)
        def _():
            pltpu.make_async_remote_copy(
                src_ref=across_source, dst_ref=across_slot(s), send_sem=across_send.at[s],
                recv_sem=across_recv.at[s], device_id=at(layer, row, col), device_id_type=MESH).wait_recv()
        inner_rows = (group * span + s) * m + layer * q + lax.broadcasted_iota(jnp.int32, (q, 1), 0)
        held = across[s * q:(s + 1) * q, :].astype(jnp.float32)
        right[s * q:(s + 1) * q, :] = jnp.where(
            jnp.logical_or(inner_rows > col_here, above), held, 0.0).astype(right.dtype)

    def products(k):
        paths = jnp.dot(left[k * q:(k + 1) * q, :], right[...], preferred_element_type=jnp.float32)
        return paths * mask_block[k * q:(k + 1) * q, :]

    in_plane = lambda l, c: pltpu.make_async_remote_copy(
        src_ref=stage.at[l], dst_ref=inbox.at[layer * cols + col], send_sem=plane_send.at[l, c],
        recv_sem=inbox_recv.at[layer * cols + col], device_id=at(l, row, c), device_id_type=MESH)
    to_self = pltpu.make_async_copy(stage.at[layer], inbox.at[layer * cols + col], keep_inbox_sem)

    def plane_sends(act, self_act):
        for l in range(layers):
            for c in range(cols):
                here = jnp.logical_and(l == layer, c == col)

                @pl.when(jnp.logical_not(here))
                def _():
                    act(in_plane(l, c))

                @pl.when(here)
                def _():
                    self_act(to_self)

    cross_slot = layers * cols + row * layers + layer
    cross = lambda s, l, c: pltpu.make_async_remote_copy(
        src_ref=cross_stage.at[s * layers + l], dst_ref=inbox.at[cross_slot],
        send_sem=cross_send.at[s * layers + l, c], recv_sem=inbox_recv.at[cross_slot],
        device_id=at(l, col * span + s, c), device_id_type=MESH)

    def cross_sends(act):
        for s in range(span):
            for l in range(layers):
                for c in range(cols):
                    act(cross(s, l, c))

    @pl.when(above)
    def _():
        total = jnp.zeros((1, n), jnp.float32)
        for k in range(layers):
            total = total + jnp.sum(products(k), axis=0, keepdims=True)
        for t in range(span * layers):
            cross_stage[t, 0:1, :] = total[:, t * q:(t + 1) * q]
            cross_stage[t, 1:2, :] = jnp.zeros((1, q), jnp.float32)
        cross_sends(lambda copy: copy.start())

    @pl.when(jnp.logical_not(above))
    def _():
        for k in range(layers):
            part = products(k)
            sums = sum(part[:, t:t + q] for t in range(0, n, q))
            stage[k, 0:1, :] = jnp.sum(sums.T, axis=0, keepdims=True)
        plane_sends(lambda copy: copy.start(), lambda copy: copy.start())

    column_sum[...] = jnp.zeros_like(column_sum)

    def take(slot):
        pltpu.make_async_remote_copy(
            src_ref=stage.at[0], dst_ref=inbox.at[slot], send_sem=plane_send.at[0, 0], recv_sem=inbox_recv.at[slot],
            device_id=at(layer, row, col), device_id_type=MESH).wait_recv()
        column_sum[...] += inbox[slot]

    for l in range(layers):
        for c in range(cols):
            here = jnp.logical_and(l == layer, c == col)

            @pl.when(jnp.logical_and(here, jnp.logical_not(above)))
            def _():
                to_self.wait()
                column_sum[...] += inbox[l * cols + c]

            @pl.when(jnp.logical_and(jnp.logical_not(here), c <= group))
            def _():
                take(l * cols + c)
    for r in range(rows):
        @pl.when(r < group * span)
        def _():
            for l in range(layers):
                take(layers * cols + r * layers + l)

    share = q // cols
    mine = jnp.zeros((2, share), jnp.float32)
    for c in range(cols):
        mine = jnp.where(c == col, column_sum[:, c * share:(c + 1) * share], mine)
    out_ref[...] = mine

    across_sends(lambda copy: copy.wait_send())
    side_sends(lambda copy: copy.wait_send())

    @pl.when(above)
    def _():
        cross_sends(lambda copy: copy.wait_send())

    @pl.when(jnp.logical_not(above))
    def _():
        plane_sends(lambda copy: copy.wait_send(), lambda copy: None)


def two_blocks(edge_weight):
    layers, rows, cols = (lax.axis_size(a) for a in ("layer", "row", "col"))
    m, n = edge_weight.shape
    q, span = m // layers, rows // cols
    slots = layers * cols + rows * layers
    dma = pltpu.SemaphoreType.DMA
    kind = edge_weight.dtype
    return pl.pallas_call(
        functools.partial(kernel, layers, rows, cols),
        out_shape=jax.ShapeDtypeStruct((2, q // cols), jnp.float32),
        in_specs=[pl.BlockSpec(memory_space=pl.ANY)],
        out_specs=pl.BlockSpec(memory_space=pltpu.VMEM),
        scratch_shapes=[
            pltpu.VMEM((m, n), kind),
            pltpu.VMEM((m, n), jnp.float32),
            pltpu.VMEM((m, span * q), kind),
            pltpu.VMEM((span * q, n), kind),
            pltpu.VMEM((m, span * q), kind),
            pltpu.VMEM((span * q, n), kind),
            pltpu.VMEM((layers, 2, q), jnp.float32),
            pltpu.VMEM((span * layers, 2, q), jnp.float32),
            pltpu.VMEM((2, q), jnp.float32),
            pltpu.VMEM((slots, 2, q), jnp.float32),
            dma, dma((span,)), dma, dma, dma((span, cols)), dma((span,)),
            dma((span,)), dma((span,)), dma((layers, cols)), dma((span * layers, cols)), dma((slots,)),
        ],
        compiler_params=pltpu.CompilerParams(collective_id=0, has_side_effects=True),
    )(edge_weight)


def three_blocks(edge_weight):
    layers, layer_index = lax.axis_size("layer"), lax.axis_index("layer")
    row_count, col_count = edge_weight.shape
    row_block = (lax.axis_index("row") * row_count + jnp.arange(row_count, dtype=jnp.int32)) // col_count
    lower = jnp.where(row_block[:, None] > lax.axis_index("col"), edge_weight, jnp.zeros_like(edge_weight))
    column_groups = lower.reshape(row_count, col_count // (STRIPE * layers), layers, STRIPE)
    left_local = lax.dynamic_index_in_dim(column_groups, layer_index, 2, keepdims=False).reshape(
        row_count, col_count // layers
    )
    row_groups = lower.reshape(row_count // (STRIPE * layers), layers, STRIPE, col_count)
    right_local = lax.dynamic_index_in_dim(row_groups, layer_index, 1, keepdims=False).reshape(
        row_count // layers, col_count
    )
    left_whole = lax.all_gather(left_local, "col", axis=1, tiled=True)
    right_whole = lax.all_gather(right_local, "row", axis=0, tiled=True)
    paths = jnp.dot(left_whole, right_whole, preferred_element_type=jnp.float32)
    triangles = jnp.sum(paths * lower, axis=1)
    layer_share = lax.psum_scatter(triangles, "layer", scatter_dimension=0, tiled=True)
    return lax.psum_scatter(layer_share, "col", scatter_dimension=0, tiled=True)


def local(edge_weight):
    sums = two_blocks(edge_weight)
    triangles, degree = sums[0], sums[1]
    if lax.axis_size("col") > 2:
        triangles = triangles + three_blocks(edge_weight)
    clustering = 2.0 * triangles / jnp.maximum(degree * (degree - 1.0), 2.0)
    return clustering.reshape(1, -1)


def solution(mesh):
    placed = (P("row", "col"),)
    return jax.shard_map(
        local, mesh=mesh, in_specs=placed, out_specs=P("row", ("layer", "col")), check_vma=False
    )
```

time: 60.6 us -> 18.7 us (0.31)
  the two profiles are of different devices: /device:TPU:0 before, /device:TPU:17 now
where the time goes in v1:
time: 18.7 us; the launch traced here: 18.6 us
  Pallas kernels  17.3 us (93%)
  other arithmetic  1.28 us (7%)
    pallas_call x1, Pallas kernels, two_blocks(): pl.pallas_call(functools.partial(kernel, layers, rows, cols), out_shape=j...  17.3 us
    div x1, other arithmetic, local(): clustering = 2.0 * triangles / jnp.maximum(degree * (degree - 1.0), 2.0)  1.28 us

profile of v1, /device:TPU:17, one launch (start us, length us, event | category | flops | bytes accessed | tf_op | source)
XLA Modules:
  0.0 18.6 jit_solution(4443496016214473089)
XLA Ops:
  0.0 17.3 %shard_map.17 = f32[2,64]{1,0:T(2,128)} custom-call(bf16[512,1024]{1,0:T(8,128)(2,1)} %w_ref.1), custom_call_target="tpu_custom_call" | custom-call | tf_op jit(solution)/shard_map/pallas_call | solution.py:258
  17.3 1.3 %fusion.1 = f32[1,64]{1,0:T(1,128)} fusion(f32[2,64]{1,0:T(2,128)} %shard_map.17), kind=kLoop, calls=%fused_computation.2 | loop fusion | flops 320 | bytes 768 | tf_op jit(solution)/shard_map/div | solution.py:307

commit v2 on v1

v2 whole, which is shorter than its diff:
```python
import functools

import jax
import jax.numpy as jnp
from jax import lax
from jax.experimental import pallas as pl
from jax.experimental.pallas import tpu as pltpu
from jax.sharding import PartitionSpec as P

STRIPE = 128
CHUNKS = 4
MESH = pl.DeviceIdType.MESH


def at(layer, row, col):
    return {"layer": layer, "row": row, "col": col}


def kernel(
    layers, rows, cols, finish, w_ref, out_ref,
    block, side, across, sums, stage, cross_stage, total, inbox,
    load_sem, keep_side_sem, keep_across_sem, keep_inbox_sem, side_send, side_recv,
    across_send, across_recv, plane_send, cross_send, inbox_recv, plane_in, above_in,
):
    span = rows // cols
    m, n = w_ref.shape
    q = m // layers
    chunk = n // CHUNKS
    layer, row, col = (lax.axis_index(a) for a in ("layer", "row", "col"))
    group = row // span
    place = row % span
    above = col > group
    diagonal = col == group
    share = jnp.where(layer % 2 == 0, layer // 2, layers - 1 - layer // 2)

    load = pltpu.make_async_copy(w_ref, block, load_sem)
    load.start()

    barrier = pltpu.get_barrier_semaphore()

    def greet(l, r, c, semaphore=barrier):
        pl.semaphore_signal(semaphore, inc=1, device_id=at(l, r, c), device_id_type=MESH)

    near = layers - 1 + cols - 1
    for c in range(cols):
        @pl.when(c != col)
        def _():
            greet(layer, row, c)
    for r in range(rows):
        is_near = jnp.logical_and(
            r != row, jnp.logical_or(r // span == group, jnp.logical_or(r == row - 1, r == row + 1)))
        near = near + jnp.where(is_near, 1, 0)

        @pl.when(is_near)
        def _():
            greet(layer, r, col)
    for l in range(layers):
        @pl.when(l != layer)
        def _():
            greet(l, row, col)

    def side_source(s, first=0):
        start = pl.multiple_of(s * m + share * q, q)
        return w_ref.at[first * q:m, pl.ds(start, q)]

    def side_slot(s, first=0):
        return side.at[first * q:m, s * q:(s + 1) * q]

    def across_source(t):
        return w_ref.at[pl.ds(pl.multiple_of(share * q, q), q), t * chunk:(t + 1) * chunk]

    def across_slot(s, t):
        return across.at[pl.ds(pl.multiple_of(s * q, q), q), t * chunk:(t + 1) * chunk]

    keep_across = pltpu.make_async_copy(
        w_ref.at[pl.ds(pl.multiple_of(share * q, q), q), :],
        across.at[pl.ds(pl.multiple_of(place * q, q), q), :], keep_across_sem)
    keep_across.start()

    def keep_side(s):
        return pltpu.make_async_copy(side_source(s), side_slot(s), keep_side_sem.at[s])

    for s in range(span):
        @pl.when(s > place)
        def _():
            side[:, s * q:(s + 1) * q] = jnp.zeros((m, q), side.dtype)
            across[s * q:(s + 1) * q, :] = jnp.zeros((q, n), across.dtype)

        @pl.when(jnp.logical_and(diagonal, s <= place))
        def _():
            keep_side(s).start()

    pl.semaphore_wait(barrier, near)

    def side_copy(s, c, first):
        return pltpu.make_async_remote_copy(
            src_ref=side_source(s, first), dst_ref=side_slot(s, first), send_sem=side_send.at[s, c],
            recv_sem=side_recv.at[s], device_id=at(layer, row, c), device_id_type=MESH)

    def side_each(s, c, act):
        @pl.when(s < place)
        def _():
            act(side_copy(s, c, 0))
        for first in range(layers):
            @pl.when(jnp.logical_and(s == place, share == first))
            def _():
                act(side_copy(s, c, first))

    def side_sends(act):
        for s in range(span):
            for c in range(cols):
                @pl.when(jnp.logical_and(diagonal, c != col))
                def _():
                    side_each(s, c, act)

    def across_copy(s, t, origin):
        return pltpu.make_async_remote_copy(
            src_ref=across_source(t), dst_ref=across_slot(origin, t), send_sem=across_send.at[s, t],
            recv_sem=across_recv.at[origin, t], device_id=at(layer, group * span + s, col), device_id_type=MESH)

    def has_entries(origin, t):
        return jnp.logical_or(jnp.logical_not(diagonal), t * chunk < (origin + 1) * m)

    def across_sends(act):
        for t in range(CHUNKS):
            for s in range(span):
                @pl.when(jnp.logical_and(s > place, has_entries(place, t)))
                def _():
                    act(across_copy(s, t, place))

    across_sends(lambda copy: copy.start())
    side_sends(lambda copy: copy.start())

    for c in range(cols):
        @pl.when(c != col)
        def _():
            greet(layer, row, c, plane_in)

    load.wait()
    per_layer = n // layers
    row_here = row * m + lax.broadcasted_iota(jnp.int32, (q, 1), 0)
    col_here = col * n + lax.broadcasted_iota(jnp.int32, (1, n), 1)

    @pl.when(diagonal)
    def _():
        for k in range(layers):
            held = block[k * q:(k + 1) * q, :].astype(jnp.float32)
            block[k * q:(k + 1) * q, :] = jnp.where(row_here + k * q > col_here, held, 0.0).astype(block.dtype)

    @pl.when(jnp.logical_not(above))
    def _():
        mine = pl.ds(pl.multiple_of(layer * per_layer, per_layer), per_layer)
        for k in range(layers):
            linked = jnp.where(block[k * q:(k + 1) * q, mine].astype(jnp.float32) > 0, 1.0, 0.0)
            counts = sum(linked[:, t:t + q] for t in range(0, per_layer, q))
            stage[k, 1:2, :] = jnp.sum(counts.T, axis=0, keepdims=True)

    pl.semaphore_wait(plane_in, cols - 1)

    @pl.when(row < rows - 1)
    def _():
        pl.semaphore_wait(above_in, 1)

    @pl.when(row > 0)
    def _():
        greet(layer, row - 1, col, above_in)

    keep_across.wait()
    for s in range(span):
        @pl.when(jnp.logical_and(diagonal, s <= place))
        def _():
            keep_side(s).wait()

        @pl.when(jnp.logical_not(diagonal))
        def _():
            side_each(s, 0, lambda copy: copy.wait_recv())

        @pl.when(s == place)
        def _():
            inner = row * m + share * q + lax.broadcasted_iota(jnp.int32, (1, q), 1)
            outer = row * m + lax.broadcasted_iota(jnp.int32, (m, 1), 0)
            held = side[:, s * q:(s + 1) * q].astype(jnp.float32)
            side[:, s * q:(s + 1) * q] = jnp.where(outer > inner, held, 0.0).astype(side.dtype)

    def operand(t):
        for s in range(span):
            @pl.when(jnp.logical_and(s < place, has_entries(s, t)))
            def _():
                across_copy(0, t, s).wait_recv()

            @pl.when(diagonal)
            def _():
                inner = (group * span + s) * m + share * q + lax.broadcasted_iota(jnp.int32, (q, 1), 0)
                outer = col * n + t * chunk + lax.broadcasted_iota(jnp.int32, (1, chunk), 1)
                held = across[s * q:(s + 1) * q, t * chunk:(t + 1) * chunk].astype(jnp.float32)
                across[s * q:(s + 1) * q, t * chunk:(t + 1) * chunk] = jnp.where(
                    inner > outer, held, 0.0).astype(across.dtype)

    def products(k, t):
        here = slice(t * chunk, (t + 1) * chunk)
        paths = jnp.dot(side[k * q:(k + 1) * q, :], across[:, here], preferred_element_type=jnp.float32)
        return paths * block[k * q:(k + 1) * q, here].astype(jnp.float32)

    in_plane = lambda l, c: pltpu.make_async_remote_copy(
        src_ref=stage.at[l], dst_ref=inbox.at[layer * cols + col], send_sem=plane_send.at[l, c],
        recv_sem=inbox_recv.at[layer * cols + col], device_id=at(l, row, c), device_id_type=MESH)
    to_self = pltpu.make_async_copy(stage.at[layer], inbox.at[layer * cols + col], keep_inbox_sem)

    def plane_sends(act, self_act):
        for l in range(layers):
            for c in range(cols):
                here = jnp.logical_and(l == layer, c == col)

                @pl.when(jnp.logical_not(here))
                def _():
                    act(in_plane(l, c))

                @pl.when(here)
                def _():
                    self_act(to_self)

    cross_slot = layers * cols + row * layers + layer
    cross = lambda s, l, c: pltpu.make_async_remote_copy(
        src_ref=cross_stage.at[s * layers + l], dst_ref=inbox.at[cross_slot],
        send_sem=cross_send.at[s * layers + l, c], recv_sem=inbox_recv.at[cross_slot],
        device_id=at(l, col * span + s, c), device_id_type=MESH)

    def cross_sends(act):
        for s in reversed(range(span)):
            for l in range(layers):
                for c in range(cols):
                    act(cross(s, l, c))

    @pl.when(above)
    def _():
        for t in range(CHUNKS):
            operand(t)
            part = sum(jnp.sum(products(k, t), axis=0, keepdims=True) for k in range(layers))
            for u in range(0, chunk, q):
                v = (t * chunk + u) // q
                cross_stage[v, 0:1, :] = part[:, u:u + q]
                cross_stage[v, 1:2, :] = jnp.zeros((1, q), jnp.float32)
        cross_sends(lambda copy: copy.start())

    @pl.when(jnp.logical_not(above))
    def _():
        for t in range(CHUNKS):
            operand(t)
            for k in range(layers):
                part = products(k, t)
                part = sum(part[:, u:u + q] for u in range(0, chunk, q))
                sums[k] = part if t == 0 else sums[k] + part
        for k in range(layers):
            stage[k, 0:1, :] = jnp.sum(sums[k].T, axis=0, keepdims=True)
        plane_sends(lambda copy: copy.start(), lambda copy: copy.start())

    total[...] = jnp.zeros_like(total)

    def take(slot):
        pltpu.make_async_remote_copy(
            src_ref=stage.at[0], dst_ref=inbox.at[slot], send_sem=plane_send.at[0, 0], recv_sem=inbox_recv.at[slot],
            device_id=at(layer, row, col), device_id_type=MESH).wait_recv()
        total[...] += inbox[slot]

    for l in range(layers):
        for c in range(cols):
            here = jnp.logical_and(l == layer, c == col)

            @pl.when(jnp.logical_and(here, jnp.logical_not(above)))
            def _():
                to_self.wait()
                total[...] += inbox[l * cols + c]

            @pl.when(jnp.logical_and(jnp.logical_not(here), c <= group))
            def _():
                take(l * cols + c)
    for r in range(rows):
        @pl.when(r < group * span)
        def _():
            for l in range(layers):
                take(layers * cols + r * layers + l)

    part = q // cols
    mine = jnp.zeros((2, part), jnp.float32)
    for c in range(cols):
        mine = jnp.where(c == col, total[:, c * part:(c + 1) * part], mine)
    out_ref[...] = clustering_of(mine[0:1], mine[1:2]) if finish else mine

    across_sends(lambda copy: copy.wait_send())
    side_sends(lambda copy: copy.wait_send())

    @pl.when(above)
    def _():
        cross_sends(lambda copy: copy.wait_send())

    @pl.when(jnp.logical_not(above))
    def _():
        plane_sends(lambda copy: copy.wait_send(), lambda copy: None)


def clustering_of(triangles, degree):
    return 2.0 * triangles / jnp.maximum(degree * (degree - 1.0), 2.0)


def two_blocks(edge_weight, finish):
    layers, rows, cols = (lax.axis_size(a) for a in ("layer", "row", "col"))
    m, n = edge_weight.shape
    q, span = m // layers, rows // cols
    slots = layers * cols + rows * layers
    dma, flag = pltpu.SemaphoreType.DMA, pltpu.SemaphoreType.REGULAR
    kind = edge_weight.dtype
    return pl.pallas_call(
        functools.partial(kernel, layers, rows, cols, finish),
        out_shape=jax.ShapeDtypeStruct((1 if finish else 2, q // cols), jnp.float32),
        in_specs=[pl.BlockSpec(memory_space=pl.ANY)],
        out_specs=pl.BlockSpec(memory_space=pltpu.VMEM),
        scratch_shapes=[
            pltpu.VMEM((m, n), kind),
            pltpu.VMEM((m, span * q), kind),
            pltpu.VMEM((span * q, n), kind),
            pltpu.VMEM((layers, q, q), jnp.float32),
            pltpu.VMEM((layers, 2, q), jnp.float32),
            pltpu.VMEM((span * layers, 2, q), jnp.float32),
            pltpu.VMEM((2, q), jnp.float32),
            pltpu.VMEM((slots, 2, q), jnp.float32),
            dma, dma((span,)), dma, dma, dma((span, cols)), dma((span,)),
            dma((span, CHUNKS)), dma((span, CHUNKS)), dma((layers, cols)), dma((span * layers, cols)), dma((slots,)),
            flag, flag,
        ],
        compiler_params=pltpu.CompilerParams(collective_id=0, has_side_effects=True),
    )(edge_weight)


def three_blocks(edge_weight):
    layers, layer_index = lax.axis_size("layer"), lax.axis_index("layer")
    row_count, col_count = edge_weight.shape
    row_block = (lax.axis_index("row") * row_count + jnp.arange(row_count, dtype=jnp.int32)) // col_count
    lower = jnp.where(row_block[:, None] > lax.axis_index("col"), edge_weight, jnp.zeros_like(edge_weight))
    column_groups = lower.reshape(row_count, col_count // (STRIPE * layers), layers, STRIPE)
    left_local = lax.dynamic_index_in_dim(column_groups, layer_index, 2, keepdims=False).reshape(
        row_count, col_count // layers
    )
    row_groups = lower.reshape(row_count // (STRIPE * layers), layers, STRIPE, col_count)
    right_local = lax.dynamic_index_in_dim(row_groups, layer_index, 1, keepdims=False).reshape(
        row_count // layers, col_count
    )
    left_whole = lax.all_gather(left_local, "col", axis=1, tiled=True)
    right_whole = lax.all_gather(right_local, "row", axis=0, tiled=True)
    paths = jnp.dot(left_whole, right_whole, preferred_element_type=jnp.float32)
    triangles = jnp.sum(paths * lower, axis=1)
    layer_share = lax.psum_scatter(triangles, "layer", scatter_dimension=0, tiled=True)
    return lax.psum_scatter(layer_share, "col", scatter_dimension=0, tiled=True)


def local(edge_weight):
    if lax.axis_size("col") == 2:
        return two_blocks(edge_weight, finish=True)
    triangles, degree = two_blocks(edge_weight, finish=False)
    return clustering_of(triangles + three_blocks(edge_weight), degree).reshape(1, -1)


def solution(mesh):
    placed = (P("row", "col"),)
    return jax.shard_map(
        local, mesh=mesh, in_specs=placed, out_specs=P("row", ("layer", "col")), check_vma=False
    )
```

time: 18.7 us -> 15.7 us (0.84)
  Pallas kernels: 17.3 us -> 14.4 us
  other arithmetic: 1.28 us -> 0 us
  local copies, waits for them, and re-layouts: 0 us -> 1.19 us
    pallas_call x1, Pallas kernels: 17.3 us -> 14.4 us  [two_blocks(): pl.pallas_call(functools.partial(kernel, layers, rows, cols, finish), out...]
    div x1 -> x0, other arithmetic: 1.28 us -> none  [local(): clustering = 2.0 * triangles / jnp.maximum(degree * (degree - 1.0), 2.0)]
    unnamed x0 -> x1, local copies, waits for them, and re-layouts: none -> 1.19 us
where the time goes in v2:
time: 15.7 us; the launch traced here: 15.6 us
  Pallas kernels  14.4 us (92%)
  local copies, waits for them, and re-layouts  1.19 us (8%)
    pallas_call x1, Pallas kernels, two_blocks(): pl.pallas_call(functools.partial(kernel, layers, rows, cols, finish), out...  14.4 us
    unnamed x1, local copies, waits for them, and re-layouts  1.19 us

profile of v2, /device:TPU:17, one launch (start us, length us, event | category | flops | bytes accessed | tf_op | source)
XLA Modules:
  0.0 15.6 jit_solution(13286240919116239206)
XLA Ops:
  0.0 14.4 %shard_map.17 = f32[1,64]{1,0:T(1,128)} custom-call(bf16[512,1024]{1,0:T(8,128)(2,1)} %w_ref.1), custom_call_target="tpu_custom_call" | custom-call | tf_op jit(solution)/shard_map/pallas_call | solution.py:312
  14.4 1.2 %copy.3 = f32[1,64]{1,0:T(1,128)} copy(f32[1,64]{1,0:T(1,128)} %shard_map.17) | data formatting | bytes 512

commit v3 on v2

--- a/solution.py
+++ b/solution.py
@@ -18,9 +18,9 @@
 
 def kernel(
     layers, rows, cols, finish, w_ref, out_ref,
-    block, side, across, sums, stage, cross_stage, total, inbox,
+    block, side, across, sums, stage, cross_stage, passed, total, inbox,
     load_sem, keep_side_sem, keep_across_sem, keep_inbox_sem, side_send, side_recv,
-    across_send, across_recv, plane_send, cross_send, inbox_recv, plane_in, above_in,
+    across_send, across_recv, pass_send, pass_recv, plane_send, cross_send, inbox_recv, plane_in, above_in,
 ):
     span = rows // cols
     m, n = w_ref.shape
@@ -147,6 +147,16 @@
             held = block[k * q:(k + 1) * q, :].astype(jnp.float32)
             block[k * q:(k + 1) * q, :] = jnp.where(row_here + k * q > col_here, held, 0.0).astype(block.dtype)
 
+    pl.semaphore_wait(plane_in, cols - 1)
+
+    @pl.when(jnp.logical_and(row >= span - 1, row < rows - 1))
+    def _():
+        pl.semaphore_wait(above_in, 1)
+
+    @pl.when(row > span - 1)
+    def _():
+        greet(layer, row - 1, col, above_in)
+
     @pl.when(jnp.logical_not(above))
     def _():
         mine = pl.ds(pl.multiple_of(layer * per_layer, per_layer), per_layer)
@@ -155,16 +165,6 @@
             counts = sum(linked[:, t:t + q] for t in range(0, per_layer, q))
             stage[k, 1:2, :] = jnp.sum(counts.T, axis=0, keepdims=True)
 
-    pl.semaphore_wait(plane_in, cols - 1)
-
-    @pl.when(row < rows - 1)
-    def _():
-        pl.semaphore_wait(above_in, 1)
-
-    @pl.when(row > 0)
-    def _():
-        greet(layer, row - 1, col, above_in)
-
     keep_across.wait()
     for s in range(span):
         @pl.when(jnp.logical_and(diagonal, s <= place))
@@ -219,7 +219,10 @@
                 def _():
                     self_act(to_self)
 
-    cross_slot = layers * cols + row * layers + layer
+    onward = pltpu.make_async_remote_copy(
+        src_ref=cross_stage, dst_ref=passed, send_sem=pass_send, recv_sem=pass_recv,
+        device_id=at(layer, jnp.minimum(row + 1, rows - 1), col), device_id_type=MESH)
+    cross_slot = layers * cols + group * layers + layer
     cross = lambda s, l, c: pltpu.make_async_remote_copy(
         src_ref=cross_stage.at[s * layers + l], dst_ref=inbox.at[cross_slot],
         send_sem=cross_send.at[s * layers + l, c], recv_sem=inbox_recv.at[cross_slot],
@@ -240,7 +243,19 @@
                 v = (t * chunk + u) // q
                 cross_stage[v, 0:1, :] = part[:, u:u + q]
                 cross_stage[v, 1:2, :] = jnp.zeros((1, q), jnp.float32)
-        cross_sends(lambda copy: copy.start())
+
+        @pl.when(place > 0)
+        def _():
+            onward.wait_recv()
+            cross_stage[...] += passed[...]
+
+        @pl.when(place < span - 1)
+        def _():
+            onward.start()
+
+        @pl.when(place == span - 1)
+        def _():
+            cross_sends(lambda copy: copy.start())
 
     @pl.when(jnp.logical_not(above))
     def _():
@@ -274,11 +289,11 @@
             @pl.when(jnp.logical_and(jnp.logical_not(here), c <= group))
             def _():
                 take(l * cols + c)
-    for r in range(rows):
-        @pl.when(r < group * span)
+    for g in range(cols):
+        @pl.when(g < group)
         def _():
             for l in range(layers):
-                take(layers * cols + r * layers + l)
+                take(layers * cols + g * layers + l)
 
     part = q // cols
     mine = jnp.zeros((2, part), jnp.float32)
@@ -289,7 +304,11 @@
     across_sends(lambda copy: copy.wait_send())
     side_sends(lambda copy: copy.wait_send())
 
-    @pl.when(above)
+    @pl.when(jnp.logical_and(above, place < span - 1))
+    def _():
+        onward.wait_send()
+
+    @pl.when(jnp.logical_and(above, place == span - 1))
     def _():
         cross_sends(lambda copy: copy.wait_send())
 
@@ -306,7 +325,7 @@
     layers, rows, cols = (lax.axis_size(a) for a in ("layer", "row", "col"))
     m, n = edge_weight.shape
     q, span = m // layers, rows // cols
-    slots = layers * cols + rows * layers
+    slots = 2 * layers * cols
     dma, flag = pltpu.SemaphoreType.DMA, pltpu.SemaphoreType.REGULAR
     kind = edge_weight.dtype
     return pl.pallas_call(
@@ -321,10 +340,11 @@
             pltpu.VMEM((layers, q, q), jnp.float32),
             pltpu.VMEM((layers, 2, q), jnp.float32),
             pltpu.VMEM((span * layers, 2, q), jnp.float32),
+            pltpu.VMEM((span * layers, 2, q), jnp.float32),
             pltpu.VMEM((2, q), jnp.float32),
             pltpu.VMEM((slots, 2, q), jnp.float32),
             dma, dma((span,)), dma, dma, dma((span, cols)), dma((span,)),
-            dma((span, CHUNKS)), dma((span, CHUNKS)), dma((layers, cols)), dma((span * layers, cols)), dma((slots,)),
+            dma((span, CHUNKS)), dma((span, CHUNKS)), dma, dma, dma((layers, cols)), dma((span * layers, cols)), dma((slots,)),
             flag, flag,
         ],
         compiler_params=pltpu.CompilerParams(collective_id=0, has_side_effects=True),

time: 15.7 us -> 15.6 us (level)
  no operation moved by 1% of the time
where the time goes in v3:
time: 15.6 us; the launch traced here: 15.5 us
  Pallas kernels  14.3 us (92%)
  local copies, waits for them, and re-layouts  1.19 us (8%)
    pallas_call x1, Pallas kernels, two_blocks(): pl.pallas_call(functools.partial(kernel, layers, rows, cols, finish), out...  14.3 us
    unnamed x1, local copies, waits for them, and re-layouts  1.19 us

profile of v3, /device:TPU:17, one launch (start us, length us, event | category | flops | bytes accessed | tf_op | source)
XLA Modules:
  0.0 15.5 jit_solution(1574480696279715144)
XLA Ops:
  0.0 14.3 %shard_map.17 = f32[1,64]{1,0:T(1,128)} custom-call(bf16[512,1024]{1,0:T(8,128)(2,1)} %w_ref.1), custom_call_target="tpu_custom_call" | custom-call | tf_op jit(solution)/shard_map/pallas_call | solution.py:331
  14.3 1.2 %copy.3 = f32[1,64]{1,0:T(1,128)} copy(f32[1,64]{1,0:T(1,128)} %shard_map.17) | data formatting | bytes 512

commit v4 on v3

--- a/solution.py
+++ b/solution.py
@@ -8,7 +8,6 @@
 from jax.sharding import PartitionSpec as P
 
 STRIPE = 128
-CHUNKS = 4
 MESH = pl.DeviceIdType.MESH
 
 
@@ -25,7 +24,7 @@
     span = rows // cols
     m, n = w_ref.shape
     q = m // layers
-    chunk = n // CHUNKS
+    chunk = n // layers
     layer, row, col = (lax.axis_index(a) for a in ("layer", "row", "col"))
     group = row // span
     place = row % span
@@ -59,12 +58,11 @@
         def _():
             greet(l, row, col)
 
-    def side_source(s, first=0):
-        start = pl.multiple_of(s * m + share * q, q)
-        return w_ref.at[first * q:m, pl.ds(start, q)]
-
-    def side_slot(s, first=0):
-        return side.at[first * q:m, s * q:(s + 1) * q]
+    def side_source(s, k):
+        return w_ref.at[k * q:(k + 1) * q, pl.ds(pl.multiple_of(s * m + share * q, q), q)]
+
+    def side_slot(s, k):
+        return side.at[k * q:(k + 1) * q, s * q:(s + 1) * q]
 
     def across_source(t):
         return w_ref.at[pl.ds(pl.multiple_of(share * q, q), q), t * chunk:(t + 1) * chunk]
@@ -78,7 +76,9 @@
     keep_across.start()
 
     def keep_side(s):
-        return pltpu.make_async_copy(side_source(s), side_slot(s), keep_side_sem.at[s])
+        return pltpu.make_async_copy(
+            w_ref.at[:, pl.ds(pl.multiple_of(s * m + share * q, q), q)], side.at[:, s * q:(s + 1) * q],
+            keep_side_sem.at[s])
 
     for s in range(span):
         @pl.when(s > place)
@@ -92,26 +92,21 @@
 
     pl.semaphore_wait(barrier, near)
 
-    def side_copy(s, c, first):
+    def side_copy(s, k, c):
         return pltpu.make_async_remote_copy(
-            src_ref=side_source(s, first), dst_ref=side_slot(s, first), send_sem=side_send.at[s, c],
-            recv_sem=side_recv.at[s], device_id=at(layer, row, c), device_id_type=MESH)
-
-    def side_each(s, c, act):
-        @pl.when(s < place)
-        def _():
-            act(side_copy(s, c, 0))
-        for first in range(layers):
-            @pl.when(jnp.logical_and(s == place, share == first))
-            def _():
-                act(side_copy(s, c, first))
+            src_ref=side_source(s, k), dst_ref=side_slot(s, k), send_sem=side_send.at[s, k, c],
+            recv_sem=side_recv.at[s, k], device_id=at(layer, row, c), device_id_type=MESH)
+
+    def side_has_entries(s, k):
+        return jnp.logical_or(s < place, jnp.logical_and(s == place, k >= share))
 
     def side_sends(act):
-        for s in range(span):
-            for c in range(cols):
-                @pl.when(jnp.logical_and(diagonal, c != col))
-                def _():
-                    side_each(s, c, act)
+        for k in range(layers):
+            for s in range(span):
+                for c in range(cols):
+                    @pl.when(jnp.logical_and(jnp.logical_and(diagonal, c != col), side_has_entries(s, k)))
+                    def _():
+                        act(side_copy(s, k, c))
 
     def across_copy(s, t, origin):
         return pltpu.make_async_remote_copy(
@@ -122,7 +117,7 @@
         return jnp.logical_or(jnp.logical_not(diagonal), t * chunk < (origin + 1) * m)
 
     def across_sends(act):
-        for t in range(CHUNKS):
+        for t in range(layers):
             for s in range(span):
                 @pl.when(jnp.logical_and(s > place, has_entries(place, t)))
                 def _():
@@ -171,18 +166,20 @@
         def _():
             keep_side(s).wait()
 
-        @pl.when(jnp.logical_not(diagonal))
-        def _():
-            side_each(s, 0, lambda copy: copy.wait_recv())
-
-        @pl.when(s == place)
-        def _():
-            inner = row * m + share * q + lax.broadcasted_iota(jnp.int32, (1, q), 1)
-            outer = row * m + lax.broadcasted_iota(jnp.int32, (m, 1), 0)
-            held = side[:, s * q:(s + 1) * q].astype(jnp.float32)
-            side[:, s * q:(s + 1) * q] = jnp.where(outer > inner, held, 0.0).astype(side.dtype)
-
-    def operand(t):
+    def side_operand(k):
+        for s in range(span):
+            @pl.when(jnp.logical_and(jnp.logical_not(diagonal), side_has_entries(s, k)))
+            def _():
+                side_copy(s, k, 0).wait_recv()
+
+            @pl.when(s == place)
+            def _():
+                inner = row * m + share * q + lax.broadcasted_iota(jnp.int32, (1, q), 1)
+                held = side[k * q:(k + 1) * q, s * q:(s + 1) * q].astype(jnp.float32)
+                side[k * q:(k + 1) * q, s * q:(s + 1) * q] = jnp.where(
+                    row_here + k * q > inner, held, 0.0).astype(side.dtype)
+
+    def across_operand(t):
         for s in range(span):
             @pl.when(jnp.logical_and(s < place, has_entries(s, t)))
             def _():
@@ -236,13 +233,15 @@
 
     @pl.when(above)
     def _():
-        for t in range(CHUNKS):
-            operand(t)
-            part = sum(jnp.sum(products(k, t), axis=0, keepdims=True) for k in range(layers))
-            for u in range(0, chunk, q):
-                v = (t * chunk + u) // q
-                cross_stage[v, 0:1, :] = part[:, u:u + q]
-                cross_stage[v, 1:2, :] = jnp.zeros((1, q), jnp.float32)
+        cross_stage[...] = jnp.zeros_like(cross_stage)
+        for shell in range(layers):
+            side_operand(shell)
+            across_operand(shell)
+            for t in range(shell + 1):
+                ks = range(shell + 1) if t == shell else [shell]
+                part = sum(jnp.sum(products(k, t), axis=0, keepdims=True) for k in ks)
+                for u in range(0, chunk, q):
+                    cross_stage[(t * chunk + u) // q, 0:1, :] += part[:, u:u + q]
 
         @pl.when(place > 0)
         def _():
@@ -259,12 +258,15 @@
 
     @pl.when(jnp.logical_not(above))
     def _():
-        for t in range(CHUNKS):
-            operand(t)
-            for k in range(layers):
-                part = products(k, t)
-                part = sum(part[:, u:u + q] for u in range(0, chunk, q))
-                sums[k] = part if t == 0 else sums[k] + part
+        for shell in range(layers):
+            side_operand(shell)
+            across_operand(shell)
+            for k in range(shell + 1):
+                part = 0.0
+                for t in range(shell + 1) if k == shell else [shell]:
+                    product = products(k, t)
+                    part = part + sum(product[:, u:u + q] for u in range(0, chunk, q))
+                sums[k] = part if k == shell else sums[k] + part
         for k in range(layers):
             stage[k, 0:1, :] = jnp.sum(sums[k].T, axis=0, keepdims=True)
         plane_sends(lambda copy: copy.start(), lambda copy: copy.start())
@@ -343,8 +345,8 @@
             pltpu.VMEM((span * layers, 2, q), jnp.float32),
             pltpu.VMEM((2, q), jnp.float32),
             pltpu.VMEM((slots, 2, q), jnp.float32),
-            dma, dma((span,)), dma, dma, dma((span, cols)), dma((span,)),
-            dma((span, CHUNKS)), dma((span, CHUNKS)), dma, dma, dma((layers, cols)), dma((span * layers, cols)), dma((slots,)),
+            dma, dma((span,)), dma, dma, dma((span, layers, cols)), dma((span, layers)),
+            dma((span, layers)), dma((span, layers)), dma, dma, dma((layers, cols)), dma((span * layers, cols)), dma((slots,)),
             flag, flag,
         ],
         compiler_params=pltpu.CompilerParams(collective_id=0, has_side_effects=True),

time: 15.6 us -> 15.8 us (1.013)
  Pallas kernels: 14.3 us -> 14.5 us
    pallas_call x1, Pallas kernels: 14.3 us -> 14.5 us  [two_blocks(): pl.pallas_call(functools.partial(kernel, layers, rows, cols, finish), out...]
where the time goes in v4:
time: 15.8 us; the launch traced here: 15.7 us
  Pallas kernels  14.5 us (92%)
  local copies, waits for them, and re-layouts  1.19 us (8%)
    pallas_call x1, Pallas kernels, two_blocks(): pl.pallas_call(functools.partial(kernel, layers, rows, cols, finish), out...  14.5 us
    unnamed x1, local copies, waits for them, and re-layouts  1.19 us

profile of v4, /device:TPU:17, one launch (start us, length us, event | category | flops | bytes accessed | tf_op | source)
XLA Modules:
  0.0 15.7 jit_solution(12546456184150414861)
XLA Ops:
  0.0 14.5 %shard_map.17 = f32[1,64]{1,0:T(1,128)} custom-call(bf16[512,1024]{1,0:T(8,128)(2,1)} %w_ref.1), custom_call_target="tpu_custom_call" | custom-call | tf_op jit(solution)/shard_map/pallas_call | solution.py:333
  14.5 1.2 %copy.3 = f32[1,64]{1,0:T(1,128)} copy(f32[1,64]{1,0:T(1,128)} %shard_map.17) | data formatting | bytes 512

commit v5 on v4

--- a/solution.py
+++ b/solution.py
@@ -17,14 +17,15 @@
 
 def kernel(
     layers, rows, cols, finish, w_ref, out_ref,
-    block, side, across, sums, stage, cross_stage, passed, total, inbox,
+    block, side, across, later_side, later_across, lend, lent, sums, stage, cross_stage, passed, total, inbox,
     load_sem, keep_side_sem, keep_across_sem, keep_inbox_sem, side_send, side_recv,
-    across_send, across_recv, pass_send, pass_recv, plane_send, cross_send, inbox_recv, plane_in, above_in,
+    across_send, across_recv, pass_send, pass_recv, lend_send, lend_recv, plane_send, cross_send, inbox_recv, plane_in, above_in,
 ):
     span = rows // cols
     m, n = w_ref.shape
     q = m // layers
     chunk = n // layers
+    split = layers // 2
     layer, row, col = (lax.axis_index(a) for a in ("layer", "row", "col"))
     group = row // span
     place = row % span
@@ -86,15 +87,19 @@
             side[:, s * q:(s + 1) * q] = jnp.zeros((m, q), side.dtype)
             across[s * q:(s + 1) * q, :] = jnp.zeros((q, n), across.dtype)
 
+        @pl.when(jnp.logical_and(s < place, jnp.logical_not(diagonal)))
+        def _():
+            across[s * q:(s + 1) * q, split * chunk:] = jnp.zeros((q, n - split * chunk), across.dtype)
+
         @pl.when(jnp.logical_and(diagonal, s <= place))
         def _():
             keep_side(s).start()
 
     pl.semaphore_wait(barrier, near)
 
-    def side_copy(s, k, c):
+    def side_copy(s, k, c, later=False):
         return pltpu.make_async_remote_copy(
-            src_ref=side_source(s, k), dst_ref=side_slot(s, k), send_sem=side_send.at[s, k, c],
+            src_ref=side_source(s, k), dst_ref=(later_side.at[s, k * q:(k + 1) * q] if later else side_slot(s, k)), send_sem=side_send.at[s, k, c],
             recv_sem=side_recv.at[s, k], device_id=at(layer, row, c), device_id_type=MESH)
 
     def side_has_entries(s, k):
@@ -108,13 +113,17 @@
                     def _():
                         act(side_copy(s, k, c))
 
-    def across_copy(s, t, origin):
+                    @pl.when(jnp.logical_and(jnp.logical_and(diagonal, c != col), s > place))
+                    def _():
+                        act(side_copy(s, k, c, True))
+
+    def across_copy(s, t, origin, later=False):
         return pltpu.make_async_remote_copy(
-            src_ref=across_source(t), dst_ref=across_slot(origin, t), send_sem=across_send.at[s, t],
+            src_ref=across_source(t), dst_ref=(later_across.at[origin, :, t * chunk:(t + 1) * chunk] if later else across_slot(origin, t)), send_sem=across_send.at[s, t],
             recv_sem=across_recv.at[origin, t], device_id=at(layer, group * span + s, col), device_id_type=MESH)
 
     def has_entries(origin, t):
-        return jnp.logical_or(jnp.logical_not(diagonal), t * chunk < (origin + 1) * m)
+        return jnp.where(diagonal, t * chunk < (origin + 1) * m, t < split)
 
     def across_sends(act):
         for t in range(layers):
@@ -123,6 +132,11 @@
                 def _():
                     act(across_copy(s, t, place))
 
+                if t >= split:
+                    @pl.when(jnp.logical_and(s < place, jnp.logical_not(diagonal)))
+                    def _():
+                        act(across_copy(s, t, place, True))
+
     across_sends(lambda copy: copy.start())
     side_sends(lambda copy: copy.start())
 
@@ -197,6 +211,22 @@
         here = slice(t * chunk, (t + 1) * chunk)
         paths = jnp.dot(side[k * q:(k + 1) * q, :], across[:, here], preferred_element_type=jnp.float32)
         return paths * block[k * q:(k + 1) * q, here].astype(jnp.float32)
+
+    def later_products(s, act):
+        @pl.when(s > place)
+        def _():
+            for k in range(layers):
+                side_copy(s, k, 0, True).wait_recv()
+            for t in range(split, layers):
+                across_copy(0, t, s, True).wait_recv()
+                here = slice(t * chunk, (t + 1) * chunk)
+                paths = lax.dot_general(
+                    later_side[s], block[:, here], (((0,), (0,)), ((), ())), preferred_element_type=jnp.float32)
+                act(t, paths * later_across[s, :, here].astype(jnp.float32))
+
+    lending = lambda s: pltpu.make_async_remote_copy(
+        src_ref=lend.at[s], dst_ref=lent.at[place], send_sem=lend_send.at[s], recv_sem=lend_recv.at[place],
+        device_id=at(layer, group * span + s, col), device_id_type=MESH)
 
     in_plane = lambda l, c: pltpu.make_async_remote_copy(
         src_ref=stage.at[l], dst_ref=inbox.at[layer * cols + col], send_sem=plane_send.at[l, c],
@@ -242,6 +272,14 @@
                 part = sum(jnp.sum(products(k, t), axis=0, keepdims=True) for k in ks)
                 for u in range(0, chunk, q):
                     cross_stage[(t * chunk + u) // q, 0:1, :] += part[:, u:u + q]
+
+        def add_columns(t, product):
+            part = jnp.sum(product, axis=0, keepdims=True)
+            for u in range(0, chunk, q):
+                cross_stage[(t * chunk + u) // q, 0:1, :] += part[:, u:u + q]
+
+        for s in range(span):
+            later_products(s, add_columns)
 
         @pl.when(place > 0)
         def _():
@@ -269,6 +307,32 @@
                 sums[k] = part if k == shell else sums[k] + part
         for k in range(layers):
             stage[k, 0:1, :] = jnp.sum(sums[k].T, axis=0, keepdims=True)
+
+        @pl.when(jnp.logical_not(diagonal))
+        def _():
+            for s in range(span):
+                def add_rows(t, product):
+                    part = sum(product[:, u:u + q] for u in range(0, chunk, q))
+                    part = jnp.sum(part.T, axis=0, keepdims=True)
+                    lend[s, 0:1, :] = part if t == split else lend[s, 0:1, :] + part
+
+                later_products(s, add_rows)
+
+                @pl.when(s > place)
+                def _():
+                    lend[s, 1:2, :] = jnp.zeros((1, q), jnp.float32)
+                    lending(s).start()
+
+                @pl.when(s < place)
+                def _():
+                    pltpu.make_async_remote_copy(
+                        src_ref=lend.at[s], dst_ref=lent.at[s], send_sem=lend_send.at[s], recv_sem=lend_recv.at[s],
+                        device_id=at(layer, row, col), device_id_type=MESH).wait_recv()
+                    for k in range(layers):
+                        @pl.when(share == k)
+                        def _():
+                            stage[k] += lent[s]
+
         plane_sends(lambda copy: copy.start(), lambda copy: copy.start())
 
     total[...] = jnp.zeros_like(total)
@@ -317,6 +381,13 @@
     @pl.when(jnp.logical_not(above))
     def _():
         plane_sends(lambda copy: copy.wait_send(), lambda copy: None)
+
+    @pl.when(col < group)
+    def _():
+        for s in range(span):
+            @pl.when(s > place)
+            def _():
+                lending(s).wait_send()
 
 
 def clustering_of(triangles, degree):
@@ -339,6 +410,10 @@
             pltpu.VMEM((m, n), kind),
             pltpu.VMEM((m, span * q), kind),
             pltpu.VMEM((span * q, n), kind),
+            pltpu.VMEM((span, m, q), kind),
+            pltpu.VMEM((span, q, n), kind),
+            pltpu.VMEM((span, 2, q), jnp.float32),
+            pltpu.VMEM((span, 2, q), jnp.float32),
             pltpu.VMEM((layers, q, q), jnp.float32),
             pltpu.VMEM((layers, 2, q), jnp.float32),
             pltpu.VMEM((span * layers, 2, q), jnp.float32),
@@ -346,7 +421,7 @@
             pltpu.VMEM((2, q), jnp.float32),
             pltpu.VMEM((slots, 2, q), jnp.float32),
             dma, dma((span,)), dma, dma, dma((span, layers, cols)), dma((span, layers)),
-            dma((span, layers)), dma((span, layers)), dma, dma, dma((layers, cols)), dma((span * layers, cols)), dma((slots,)),
+            dma((span, layers)), dma((span, layers)), dma, dma, dma((span,)), dma((span,)), dma((layers, cols)), dma((span * layers, cols)), dma((slots,)),
             flag, flag,
         ],
         compiler_params=pltpu.CompilerParams(collective_id=0, has_side_effects=True),

time: 15.8 us -> 17.3 us (1.095)
  the two profiles are of different devices: /device:TPU:17 before, /device:TPU:25 now
where the time goes in v5:
time: 17.3 us; the launch traced here: 17.2 us
  Pallas kernels  16 us (92%)
  local copies, waits for them, and re-layouts  1.19 us (7%)
    pallas_call x1, Pallas kernels, two_blocks(): pl.pallas_call(functools.partial(kernel, layers, rows, cols, finish), out...  16 us
    unnamed x1, local copies, waits for them, and re-layouts  1.19 us

profile of v5, /device:TPU:25, one launch (start us, length us, event | category | flops | bytes accessed | tf_op | source)
XLA Modules:
  0.0 17.2 jit_solution(7376501225361114050)
XLA Ops:
  0.0 16.0 %shard_map.17 = f32[1,64]{1,0:T(1,128)} custom-call(bf16[512,1024]{1,0:T(8,128)(2,1)} %w_ref.1), custom_call_target="tpu_custom_call" | custom-call | tf_op jit(solution)/shard_map/pallas_call | solution.py:404
  16.0 1.2 %copy.3 = f32[1,64]{1,0:T(1,128)} copy(f32[1,64]{1,0:T(1,128)} %shard_map.17) | data formatting | bytes 512

commit v6 on v4

--- a/solution.py
+++ b/solution.py
@@ -144,11 +144,11 @@
 
     pl.semaphore_wait(plane_in, cols - 1)
 
-    @pl.when(jnp.logical_and(row >= span - 1, row < rows - 1))
+    @pl.when(jnp.logical_and(col > 0, jnp.logical_and(row >= span - 1, row < rows - 1)))
     def _():
         pl.semaphore_wait(above_in, 1)
 
-    @pl.when(row > span - 1)
+    @pl.when(jnp.logical_and(col > 0, row > span - 1))
     def _():
         greet(layer, row - 1, col, above_in)
 
@@ -332,7 +332,7 @@
     kind = edge_weight.dtype
     return pl.pallas_call(
         functools.partial(kernel, layers, rows, cols, finish),
-        out_shape=jax.ShapeDtypeStruct((1 if finish else 2, q // cols), jnp.float32),
+        out_shape=pltpu.VMEM((1 if finish else 2, q // cols), jnp.float32),
         in_specs=[pl.BlockSpec(memory_space=pl.ANY)],
         out_specs=pl.BlockSpec(memory_space=pltpu.VMEM),
         scratch_shapes=[

time: 15.8 us -> 14.6 us (0.924)
  local copies, waits for them, and re-layouts: 1.19 us -> 0.51 us
  Pallas kernels: 14.5 us -> 13.9 us
    unnamed x1, local copies, waits for them, and re-layouts: 1.19 us -> 0.51 us
    pallas_call x1, Pallas kernels: 14.5 us -> 13.9 us  [two_blocks(): pl.pallas_call(functools.partial(kernel, layers, rows, cols, finish), out...]
where the time goes in v6:
time: 14.6 us; the launch traced here: 14.4 us
  Pallas kernels  13.9 us (95%)
  local copies, waits for them, and re-layouts  0.51 us (3%)
    pallas_call x1, Pallas kernels, two_blocks(): pl.pallas_call(functools.partial(kernel, layers, rows, cols, finish), out...  13.9 us
    unnamed x1, local copies, waits for them, and re-layouts  0.51 us

profile of v6, /device:TPU:17, one launch (start us, length us, event | category | flops | bytes accessed | tf_op | source)
XLA Modules:
  0.0 14.4 jit_solution(8669290343744454046)
XLA Ops:
  0.0 13.9 %shard_map.17 = f32[1,64]{1,0:T(1,128)S(1)} custom-call(bf16[512,1024]{1,0:T(8,128)(2,1)} %w_ref.1), custom_call_target="tpu_custom_call" | custom-call | tf_op jit(solution)/shard_map/pallas_call | solution.py:333
  13.9 0.5 %copy.3 = f32[1,64]{1,0:T(1,128)} copy(f32[1,64]{1,0:T(1,128)S(1)} %shard_map.17) | data formatting | bytes 512
